TPU v7x, 32 devices: a whole 2x2x4 slice. The times are simulated.
32 devices in a mesh: tower: 2 (over core), depth: 4 (over z), sub: 4 (over y, x).
Axes of the slice: x: 2, y: 2, z: 4, core: 2. Of those that a mesh axis runs over, the one named last changes fastest.
Arguments:
- embeds: bfloat16 [2, 16384, 1024], P('tower', ('depth', 'sub')), may hold values from -700 to 700
- counts: int32 [16], P(('depth', 'sub')), may hold values from 256 to 1024, as said below
Outputs:
- row_grads: bfloat16 [2, 16384, 1024], P('tower', ('depth', 'sub'))
- corr_mean: float32 [], replicated
Inputs may be any that keep to these rules, and one draw needn't show every extreme that they name: `counts`: block b holds at least 256 and at most 256 + 768 * b // 15 valid samples; the first block holds exactly 256 and the last block is full.
All inputs are finite; a program needn't handle non-finite values.
Results may differ from a plain program's by a relative error of at most 0.022.
Values may be sent and summed in bfloat16 or wider, within the bound.
No kernel may reach another device: no remote copies, remote signals or barrier semaphores. Data moves between devices by JAX's collectives and lax.ppermute only.
A program may use at most 128 MiB of HBM per device.

v0:
```python
import jax
import jax.numpy as jnp
from jax import lax
from jax.sharding import PartitionSpec as P

REG = 0.001
contract_rows = (((0,), (0,)), ((), ()))


def from_partner(value, axis, apart):
    mask = 2**apart
    pairs = [(source, source ^ mask) for source in range(lax.axis_size(axis))]
    return lax.ppermute(value, axis, pairs)


def whitening(block_rows, valid_rows, gram_total, column_sum, count_total):
    feature_width = block_rows.shape[1]
    column_mean = column_sum / count_total
    covariance = (gram_total - jnp.outer(column_sum, column_mean)) / (
        count_total - 1.0
    ) + REG * jnp.eye(feature_width, dtype=jnp.float32)
    factor_lower = jnp.linalg.cholesky(covariance)
    centered = jnp.where(
        valid_rows[:, None], block_rows.astype(jnp.float32) - column_mean[None, :], 0.0
    )
    whitened = jax.scipy.linalg.solve_triangular(factor_lower, centered.T, lower=True).T
    return (whitened.astype(jnp.bfloat16), factor_lower)


def gradient_rows(own_white, other_white, turned, factor_lower, valid_rows):
    product_rows = jnp.dot(own_white, turned, preferred_element_type=jnp.float32)
    residual = (other_white.astype(jnp.float32) - product_rows).astype(jnp.bfloat16)
    back_rows = lax.dot_general(
        residual, turned, (((1,), (1,)), ((), ())), preferred_element_type=jnp.float32
    )
    solved = jax.scipy.linalg.solve_triangular(factor_lower, back_rows.T, lower=True, trans=1).T
    return jnp.where(valid_rows[:, None], solved, 0.0).astype(jnp.bfloat16)


def on_device(embeds, counts):
    block_rows = embeds[0]
    rows_local = block_rows.shape[0]
    feature_width = block_rows.shape[1]
    valid_rows = lax.iota(jnp.int32, rows_local) < counts[0]
    log_tower = lax.axis_index("tower") == 0
    count_part = counts.astype(jnp.float32)
    masked = jnp.where(valid_rows[:, None], block_rows, jnp.zeros_like(block_rows))
    gram_part = lax.dot_general(masked, masked, contract_rows, preferred_element_type=jnp.float32)
    column_part = jnp.sum(masked, axis=0, dtype=jnp.float32)
    gram_total, column_sum, count_sums = lax.psum(
        (gram_part, column_part, count_part), ("depth", "sub")
    )
    count_total = count_sums[0]
    whitened, factor_lower = whitening(block_rows, valid_rows, gram_total, column_sum, count_total)
    partner_rows = from_partner(whitened, "tower", 0)
    log_white = jnp.where(log_tower, whitened, partner_rows)
    image_white = jnp.where(log_tower, partner_rows, whitened)
    half_rows = rows_local // 2
    first_row = lax.axis_index("tower") * half_rows
    log_part = lax.dynamic_slice_in_dim(log_white, first_row, half_rows, 0)
    image_part = lax.dynamic_slice_in_dim(image_white, first_row, half_rows, 0)
    group_size = lax.axis_size(("tower", "depth", "sub"))
    cross_part = lax.dot_general(
        log_part, image_part, contract_rows, preferred_element_type=jnp.float32
    )
    cross_share = lax.psum_scatter(
        cross_part.reshape(group_size, -1),
        ("tower", "depth", "sub"),
        scatter_dimension=0,
        tiled=True,
    )
    share_bf = (cross_share / (count_total - 1.0)).astype(jnp.bfloat16)
    gathered = lax.all_gather(share_bf, ("tower", "depth", "sub"), axis=0, tiled=True)
    cross_bf = gathered.reshape(feature_width, feature_width)
    corr_mean = jnp.sum(jnp.square(cross_bf.astype(jnp.float32))) / feature_width
    turned = jnp.where(log_tower, cross_bf, cross_bf.T)
    gradient = gradient_rows(whitened, partner_rows, turned, factor_lower, valid_rows)
    return (gradient[None], corr_mean)


def solution(mesh):
    placed = (P("tower", ("depth", "sub"), None), P(("depth", "sub")))
    return jax.shard_map(
        on_device,
        mesh=mesh,
        in_specs=placed,
        out_specs=(P("tower", ("depth", "sub"), None), P()),
        check_vma=False,
    )
```

profile of v0, /device:TPU:0, one launch (start us, length us, event | category | flops | bytes accessed | tf_op | source)
XLA Modules:
  0.0 871.4 jit_solution(1099078158956488727)
XLA Ops:
  7.9 6.7 fusion.19
  18.0 47.7 %all-reduce.2 = (f32[1024]{0:T(1024)S(1)}, f32[]{:T(128)}) all-reduce(f32[1024]{0:T(1024)S(1)} %convert_reduce_fusion, f32[]{:T(128)} %bitcast.3), channel_id=1, replica_groups=mesh['tower'=2,'depth'=4,'sub'=4] {'depth','sub'}, use_global_device_ids=true, to_apply=%region_2.3 | all-reduce | flops 1025 | bytes 8200 | tf_op jit(solution)/shard_map/psum | solution.py:50
  67.0 120.0 %all-reduce.6.cloned.1.call-done = f32[1024,1024]{0,1:T(8,128)} async-done(((f32[1024,1024]{0,1:T(8,128)}), f32[1024,1024]{0,1:T(8,128)}) %all-reduce.6.cloned.1.call-update) | async-done | bytes 4194320 | tf_op jit(solution)/shard_map/psum | solution.py:50
  187.0 5.7 select_add_fusion
  192.7 5.5 copy.62
  198.3 4.4 fusion
  204.6 11.7 %cholesky.222 = f32[128,128]{1,0:T(8,128)S(1)} custom-call(f32[128,128]{1,0:T(8,128)S(1)} %cholesky.577), custom_call_target="Cholesky" | custom-call | tf_op jit(solution)/shard_map/jit(cholesky)/cholesky | solution.py:22
  216.4 9.8 %custom-call.66 = f32[1,128,128]{1,2,0:T(8,128)S(1)} custom-call(f32[1,128,128]{2,1,0:T(8,128)S(1)} %get-tuple-element.64), custom_call_target="InvertDiagBlocksLowerTriangular" | custom-call | tf_op jit(solution)/shard_map/jit(cholesky)/cholesky | solution.py:22
  229.3 11.7 %cholesky.243 = f32[128,128]{1,0:T(8,128)S(1)} custom-call(f32[128,128]{1,0:T(8,128)S(1)} %cholesky.581), custom_call_target="Cholesky" | custom-call | tf_op jit(solution)/shard_map/jit(cholesky)/cholesky | solution.py:22
  241.8 9.8 %custom-call.67 = f32[1,128,128]{1,2,0:T(8,128)S(1)} custom-call(f32[1,128,128]{2,1,0:T(8,128)S(1)} %get-tuple-element.62), custom_call_target="InvertDiagBlocksLowerTriangular" | custom-call | tf_op jit(solution)/shard_map/jit(cholesky)/cholesky | solution.py:22
  257.2 11.7 %cholesky.466 = f32[128,128]{1,0:T(8,128)S(1)} custom-call(f32[128,128]{1,0:T(8,128)S(1)} %cholesky.586), custom_call_target="Cholesky" | custom-call | tf_op jit(solution)/shard_map/jit(cholesky)/cholesky | solution.py:22
  269.7 9.8 %custom-call.68 = f32[1,128,128]{1,2,0:T(8,128)S(1)} custom-call(f32[1,128,128]{2,1,0:T(8,128)S(1)} %get-tuple-element.60), custom_call_target="InvertDiagBlocksLowerTriangular" | custom-call | tf_op jit(solution)/shard_map/jit(cholesky)/cholesky | solution.py:22
  284.0 11.7 %cholesky.485 = f32[128,128]{1,0:T(8,128)S(1)} custom-call(f32[128,128]{1,0:T(8,128)S(1)} %cholesky.591), custom_call_target="Cholesky" | custom-call | tf_op jit(solution)/shard_map/jit(cholesky)/cholesky | solution.py:22
  296.5 9.8 %custom-call.69 = f32[1,128,128]{1,2,0:T(8,128)S(1)} custom-call(f32[1,128,128]{2,1,0:T(8,128)S(1)} %get-tuple-element.58), custom_call_target="InvertDiagBlocksLowerTriangular" | custom-call | tf_op jit(solution)/shard_map/jit(cholesky)/cholesky | solution.py:22
  310.6 12.1 %cholesky.504 = f32[128,128]{1,0:T(8,128)S(1)} custom-call(f32[128,128]{1,0:T(8,128)S(1)} %cholesky.596), custom_call_target="Cholesky" | custom-call | tf_op jit(solution)/shard_map/jit(cholesky)/cholesky | solution.py:22
  323.5 9.8 %custom-call.70 = f32[1,128,128]{1,2,0:T(8,128)S(1)} custom-call(f32[1,128,128]{2,1,0:T(8,128)S(1)} %get-tuple-element.56), custom_call_target="InvertDiagBlocksLowerTriangular" | custom-call | tf_op jit(solution)/shard_map/jit(cholesky)/cholesky | solution.py:22
  337.7 11.7 %cholesky.524 = f32[128,128]{1,0:T(8,128)S(1)} custom-call(f32[128,128]{1,0:T(8,128)S(1)} %cholesky.601), custom_call_target="Cholesky" | custom-call | tf_op jit(solution)/shard_map/jit(cholesky)/cholesky | solution.py:22
  350.2 9.8 %custom-call.71 = f32[1,128,128]{1,2,0:T(8,128)S(1)} custom-call(f32[1,128,128]{2,1,0:T(8,128)S(1)} %get-tuple-element.54), custom_call_target="InvertDiagBlocksLowerTriangular" | custom-call | tf_op jit(solution)/shard_map/jit(cholesky)/cholesky | solution.py:22
  363.9 11.7 %cholesky.544 = f32[128,128]{1,0:T(8,128)S(1)} custom-call(f32[128,128]{1,0:T(8,128)S(1)} %cholesky.606), custom_call_target="Cholesky" | custom-call | tf_op jit(solution)/shard_map/jit(cholesky)/cholesky | solution.py:22
  376.3 9.8 %custom-call.72 = f32[1,128,128]{1,2,0:T(8,128)S(1)} custom-call(f32[1,128,128]{2,1,0:T(8,128)S(1)} %get-tuple-element.52), custom_call_target="InvertDiagBlocksLowerTriangular" | custom-call | tf_op jit(solution)/shard_map/jit(cholesky)/cholesky | solution.py:22
  389.3 11.7 %cholesky.562 = f32[128,128]{1,0:T(8,128)S(1)} custom-call(f32[128,128]{1,0:T(8,128)S(1)} %convolution_subtract_fusion.11), custom_call_target="Cholesky" | custom-call | tf_op jit(solution)/shard_map/jit(cholesky)/cholesky | solution.py:22
  411.4 4.8 select_select_fusion
  416.2 28.3 %while.1 = (s32[]{:T(128)}, f32[1024,1024]{0,1:T(8,128)}, s32[8,2]{0,1:T(2,128)S(1)}, f32[8,128,128]{2,1,0:T(8,128)}, s32[]{:T(128)}) while((s32[]{:T(128)}, f32[1024,1024]{0,1:T(8,128)}, s32[8,2]{0,1:T(2,128)S(1)}, f32[8,128,128]{2,1,0:T(8,128)}, s32[]{:T(128)}) %tuple.57), condition=%wide.while_cond, body=%wide.while_body.sunk | while | flops 2 | bytes 393829 | solution.py:36
  444.5 79.8 %custom-call.73 = f32[8,128,128]{1,2,0:T(8,128)S(1)} custom-call(f32[8,128,128]{2,1,0:T(8,128)} %get-tuple-element.9), custom_call_target="InvertDiagBlocksLowerTriangular" | custom-call | tf_op jit(solution)/shard_map/jit(_solve_triangular)/triangular_solve | solution.py:36
  552.9 5.0 fusion.50
  557.9 5.0 reshape.131
  562.9 141.7 %all-reduce.8.cloned.1.call-done = f32[32,32768]{1,0:T(8,128)} async-done(((f32[32,32768]{1,0:T(8,128)}), f32[32,32768]{1,0:T(8,128)}) %all-reduce.8.cloned.1.call-update) | async-done | bytes 4194320
  706.7 62.5 %all-gather.3.cloned.1.call-done = bf16[32,1,32768]{2,1,0:T(2,128)(2,1)} async-done(((bf16[1,1,32768]{2,1,0:T(2,128)(2,1)}), bf16[32,1,32768]{2,1,0:T(2,128)(2,1)}) %all-gather.3.cloned.1.call-update) | async-done | bytes 2097168 | tf_op jit(solution)/shard_map/all_gather | solution.py:73
  769.2 12.5 %reduce.50 = bf16[32,32768]{1,0:T(8,128)(2,1)S(1)} reduce(bf16[32,1,32768]{2,1,0:T(2,128)(2,1)} %all-gather.3.cloned.1.call-done, bf16[]{:T(256)} %constant.330), dimensions={1}, to_apply=%all-gather.reduce_sub_computation | reduce | bytes 4194306 | tf_op jit(solution)/shard_map/all_gather | solution.py:73
  788.2 10.1 %fusion.1 = f32[1024,1024]{1,0:T(8,128)} fusion(bf16[1024,1024]{0,1:T(8,128)(2,1)} %collective-permute-done, bf16[1024,1024]{0,1:T(8,128)(2,1)} %copy.79, bf16[1024,1024]{1,0:T(8,128)(2,1)S(1)} %copy-done.4, pred[]{:T(512)S(6)} %eq.7, bf16[1024,1024]{1,0:T(8,128)(2,1)} %copy-done.5), kind=kOutput, calls=%fused_computation.13 | convolution fusion | flops 4300210176 | bytes 12582913 | tf_op jit(solution)/shard_map/dot_general | solution.py:33
  840.4 4.5 fusion.72
  853.2 9.5 %multiply_reduce_fusion = f32[]{:T(128)} fusion(bf16[32,1,32768]{2,1,0:T(2,128)(2,1)S(1)} %copy-done.1), kind=kLoop, calls=%fused_computation.5 | loop fusion | flops 3145727 | bytes 2097156 | tf_op jit(solution)/shard_map/reduce_sum | solution.py:75
  (200 shorter events, 160.2 us)
Async XLA Ops:
  7.2 179.9 %all-reduce.6.cloned.1.call-start = ((), (), s32[]{:S(2)}) async-start(), calls=%async_computation | async-start | bytes 8388608 | tf_op jit(solution)/shard_map/psum | solution.py:50
  14.6 690.1 %all-reduce.8.cloned.1.call-start = ((), (), s32[]{:S(2)}) async-start(), calls=%async_computation.2 | async-start | bytes 8388608
  202.7 1.9 copy-start.3
  252.8 2.0 copy-start
  524.4 291.3 %copy-start.6 = (f32[8,128,128]{1,2,0:T(8,128)}, f32[8,128,128]{1,2,0:T(8,128)S(1)}, u32[]{:S(2)}) copy-start(f32[8,128,128]{1,2,0:T(8,128)S(1)} %custom-call.73) | copy-start | bytes 1572868
  524.4 4.5 copy-start.2
  548.5 9.4 %copy-start.5 = (bf16[1024,1024]{1,0:T(8,128)(2,1)}, bf16[1024,1024]{1,0:T(8,128)(2,1)S(1)}, u32[]{:S(2)}) copy-start(bf16[1024,1024]{1,0:T(8,128)(2,1)S(1)} %fusion.41) | copy-start | bytes 6291460
  548.5 4.4 collective-permute-start
  562.9 206.3 %all-gather.3.cloned.1.call-start = ((), (), s32[]{:S(2)}) async-start(), calls=%async_computation.1 | async-start | bytes 4325376 | tf_op jit(solution)/shard_map/all_gather | solution.py:73
  784.1 4.1 copy-start.4
  840.3 10.6 %copy-start.10 = (bf16[128,1024]{0,1:T(8,128)(2,1)S(1)}, bf16[128,1024]{0,1:T(8,128)(2,1)}, u32[]{:S(2)}) copy-start(bf16[128,1024]{0,1:T(8,128)(2,1)} %copy.84) | copy-start | bytes 786436
  840.3 10.7 %copy-start.9 = (bf16[128,1024]{0,1:T(8,128)(2,1)S(1)}, bf16[128,1024]{0,1:T(8,128)(2,1)}, u32[]{:S(2)}) copy-start(bf16[128,1024]{0,1:T(8,128)(2,1)} %copy.85) | copy-start | bytes 786436
  840.3 10.8 %copy-start.8 = (bf16[128,1024]{0,1:T(8,128)(2,1)S(1)}, bf16[128,1024]{0,1:T(8,128)(2,1)}, u32[]{:S(2)}) copy-start(bf16[128,1024]{0,1:T(8,128)(2,1)} %copy.86) | copy-start | bytes 786436
  840.3 10.9 %copy-start.7 = (bf16[128,1024]{0,1:T(8,128)(2,1)S(1)}, bf16[128,1024]{0,1:T(8,128)(2,1)}, u32[]{:S(2)}) copy-start(bf16[128,1024]{0,1:T(8,128)(2,1)} %copy.87) | copy-start | bytes 786436
  849.8 3.5 copy-start.1
Sparse Core Ops, SparseCore 0:
  14.7 172.2 all-reduce.5
  563.0 141.6 all-reduce.7
  708.2 60.9 all-gather.2
where the time goes:
time: 877 us; the launch traced here: 871 us
  waiting for transfers between devices  329 us (38%)
  other arithmetic  289 us (33%)
  matrix products  106 us (12%)
  local copies, waits for them, and re-layouts  77.1 us (9%)
  blocking collectives  47.7 us (5%)
  between operations  23 us (3%)
    another operation x30, other arithmetic, whitening(): factor_lower = jnp.linalg.cholesky(covariance)  168 us
    unnamed x4, waiting for transfers between devices  142 us
    psum x1, waiting for transfers between devices, on_device(): lax.psum((gram_part, column_part, count_part), ('depth', 'sub'))  120 us
    another operation x3, other arithmetic, gradient_rows(): jax.scipy.linalg.solve_triangular(factor_lower, back_rows.T, lower=True,...  84.6 us
    all_gather x1, waiting for transfers between devices, on_device(): lax.all_gather(share_bf, ('tower', 'depth', 'sub'), axis=0, tiled=True)  62.5 us
    psum x1, blocking collectives, on_device(): lax.psum((gram_part, column_part, count_part), ('depth', 'sub'))  47.7 us
    another operation x15, matrix products, gradient_rows(): jax.scipy.linalg.solve_triangular(factor_lower, back_rows.T, lower=True,...  34.7 us
    another operation x40, local copies, waits for them, and re-layouts  28.2 us
  transfers between devices with their start and end apart: 4, of which 4 were waited for; matrix products, arithmetic and copies ran while one was open for 0% of the time, Pallas kernels for 0%

commit v1 on v0

--- a/solution.py
+++ b/solution.py
@@ -70,7 +70,20 @@
         tiled=True,
     )
     share_bf = (cross_share / (count_total - 1.0)).astype(jnp.bfloat16)
-    gathered = lax.all_gather(share_bf, ("tower", "depth", "sub"), axis=0, tiled=True)
+    ways, here = (
+        lax.axis_size(("tower", "depth", "sub")),
+        lax.axis_index(("tower", "depth", "sub")),
+    )
+    grown, reach = (share_bf, 1)
+    while reach < ways:
+        theirs = lax.ppermute(
+            grown, ("tower", "depth", "sub"), [(d, d ^ reach) for d in range(ways)]
+        )
+        mine_first = jnp.concatenate([grown, theirs], axis=0)
+        theirs_first = jnp.concatenate([theirs, grown], axis=0)
+        grown = jnp.where(here & reach == 0, mine_first, theirs_first)
+        reach = 2 * reach
+    gathered = grown
     cross_bf = gathered.reshape(feature_width, feature_width)
     corr_mean = jnp.sum(jnp.square(cross_bf.astype(jnp.float32))) / feature_width
     turned = jnp.where(log_tower, cross_bf, cross_bf.T)

time: 877 us -> 832 us (0.949)
  waiting for transfers between devices: 329 us -> 301 us
  other arithmetic: 289 us -> 270 us
    all_gather x1 -> x0, waiting for transfers between devices: 62.5 us -> none  [on_device(): lax.all_gather(share_bf, ('tower', 'depth', 'sub'), axis=0, tiled=True)]
    ppermute x0 -> x5, waiting for transfers between devices: none -> 35.2 us  [on_device(): lax.ppermute(grown, ('tower', 'depth', 'sub'), [(d, d ^ reach) for d in r...]
    all_gather x1 -> x0, other arithmetic: 12.5 us -> none  [on_device(): lax.all_gather(share_bf, ('tower', 'depth', 'sub'), axis=0, tiled=True)]
    unnamed x4 -> x3, waiting for transfers between devices: 142 us -> 142 us
  transfers between devices with their start and end apart: 4 -> 8, of which waited for: 4 -> 8; matrix products, arithmetic and copies ran while one was open for 0% -> 0% of each run, Pallas kernels for 0% -> 0%
where the time goes in v1:
time: 832 us; the launch traced here: 826 us
  waiting for transfers between devices  301 us (36%)
  other arithmetic  270 us (32%)
  matrix products  106 us (13%)
  local copies, waits for them, and re-layouts  72.7 us (9%)
  blocking collectives  47.7 us (6%)
  between operations  23.2 us (3%)
    another operation x30, other arithmetic, whitening(): factor_lower = jnp.linalg.cholesky(covariance)  167 us
    unnamed x3, waiting for transfers between devices  142 us
    psum x1, waiting for transfers between devices, on_device(): lax.psum((gram_part, column_part, count_part), ('depth', 'sub'))  120 us
    another operation x3, other arithmetic, gradient_rows(): jax.scipy.linalg.solve_triangular(factor_lower, back_rows.T, lower=True,...  83.6 us
    psum x1, blocking collectives, on_device(): lax.psum((gram_part, column_part, count_part), ('depth', 'sub'))  47.7 us
    ppermute x5, waiting for transfers between devices, on_device(): lax.ppermute(grown, ('tower', 'depth', 'sub'), [(d, d ^ reach) for d in r...  35.2 us
    another operation x15, matrix products, gradient_rows(): jax.scipy.linalg.solve_triangular(factor_lower, back_rows.T, lower=True,...  34.7 us
    another operation x14, matrix products, whitening(): factor_lower = jnp.linalg.cholesky(covariance)  26.6 us
  transfers between devices with their start and end apart: 8, of which 8 were waited for; matrix products, arithmetic and copies ran while one was open for 0% of the time, Pallas kernels for 0%

profile of v1, /device:TPU:0, one launch (start us, length us, event | category | flops | bytes accessed | tf_op | source)
XLA Modules:
  0.0 826.2 jit_solution(9911768373295503937)
XLA Ops:
  7.9 6.7 fusion.19
  18.0 47.7 %all-reduce.2 = (f32[1024]{0:T(1024)S(1)}, f32[]{:T(128)}) all-reduce(f32[1024]{0:T(1024)S(1)} %convert_reduce_fusion, f32[]{:T(128)} %bitcast.3), channel_id=1, replica_groups=mesh['tower'=2,'depth'=4,'sub'=4] {'depth','sub'}, use_global_device_ids=true, to_apply=%region_2.3 | all-reduce | flops 1025 | bytes 8200 | tf_op jit(solution)/shard_map/psum | solution.py:50
  67.0 120.1 %all-reduce.6.cloned.1.call-done = f32[1024,1024]{0,1:T(8,128)} async-done(((f32[1024,1024]{0,1:T(8,128)}), f32[1024,1024]{0,1:T(8,128)}) %all-reduce.6.cloned.1.call-update) | async-done | bytes 4194320 | tf_op jit(solution)/shard_map/psum | solution.py:50
  187.1 5.7 select_add_fusion
  192.8 5.5 copy.34
  198.3 4.4 fusion
  204.7 11.7 %cholesky.222 = f32[128,128]{1,0:T(8,128)S(1)} custom-call(f32[128,128]{1,0:T(8,128)S(1)} %cholesky.577), custom_call_target="Cholesky" | custom-call | tf_op jit(solution)/shard_map/jit(cholesky)/cholesky | solution.py:22
  216.4 9.8 %custom-call.66 = f32[1,128,128]{1,2,0:T(8,128)S(1)} custom-call(f32[1,128,128]{2,1,0:T(8,128)S(1)} %get-tuple-element.62), custom_call_target="InvertDiagBlocksLowerTriangular" | custom-call | tf_op jit(solution)/shard_map/jit(cholesky)/cholesky | solution.py:22
  229.3 11.7 %cholesky.243 = f32[128,128]{1,0:T(8,128)S(1)} custom-call(f32[128,128]{1,0:T(8,128)S(1)} %cholesky.581), custom_call_target="Cholesky" | custom-call | tf_op jit(solution)/shard_map/jit(cholesky)/cholesky | solution.py:22
  241.7 9.8 %custom-call.67 = f32[1,128,128]{1,2,0:T(8,128)S(1)} custom-call(f32[1,128,128]{2,1,0:T(8,128)S(1)} %get-tuple-element.60), custom_call_target="InvertDiagBlocksLowerTriangular" | custom-call | tf_op jit(solution)/shard_map/jit(cholesky)/cholesky | solution.py:22
  257.0 11.7 %cholesky.466 = f32[128,128]{1,0:T(8,128)S(1)} custom-call(f32[128,128]{1,0:T(8,128)S(1)} %cholesky.586), custom_call_target="Cholesky" | custom-call | tf_op jit(solution)/shard_map/jit(cholesky)/cholesky | solution.py:22
  269.5 9.8 %custom-call.68 = f32[1,128,128]{1,2,0:T(8,128)S(1)} custom-call(f32[1,128,128]{2,1,0:T(8,128)S(1)} %get-tuple-element.58), custom_call_target="InvertDiagBlocksLowerTriangular" | custom-call | tf_op jit(solution)/shard_map/jit(cholesky)/cholesky | solution.py:22
  284.1 11.7 %cholesky.485 = f32[128,128]{1,0:T(8,128)S(1)} custom-call(f32[128,128]{1,0:T(8,128)S(1)} %cholesky.591), custom_call_target="Cholesky" | custom-call | tf_op jit(solution)/shard_map/jit(cholesky)/cholesky | solution.py:22
  296.6 9.8 %custom-call.69 = f32[1,128,128]{1,2,0:T(8,128)S(1)} custom-call(f32[1,128,128]{2,1,0:T(8,128)S(1)} %get-tuple-element.56), custom_call_target="InvertDiagBlocksLowerTriangular" | custom-call | tf_op jit(solution)/shard_map/jit(cholesky)/cholesky | solution.py:22
  310.7 11.9 %cholesky.504 = f32[128,128]{1,0:T(8,128)S(1)} custom-call(f32[128,128]{1,0:T(8,128)S(1)} %cholesky.596), custom_call_target="Cholesky" | custom-call | tf_op jit(solution)/shard_map/jit(cholesky)/cholesky | solution.py:22
  323.3 9.8 %custom-call.70 = f32[1,128,128]{1,2,0:T(8,128)S(1)} custom-call(f32[1,128,128]{2,1,0:T(8,128)S(1)} %get-tuple-element.54), custom_call_target="InvertDiagBlocksLowerTriangular" | custom-call | tf_op jit(solution)/shard_map/jit(cholesky)/cholesky | solution.py:22
  337.5 11.7 %cholesky.524 = f32[128,128]{1,0:T(8,128)S(1)} custom-call(f32[128,128]{1,0:T(8,128)S(1)} %cholesky.601), custom_call_target="Cholesky" | custom-call | tf_op jit(solution)/shard_map/jit(cholesky)/cholesky | solution.py:22
  350.0 9.8 %custom-call.71 = f32[1,128,128]{1,2,0:T(8,128)S(1)} custom-call(f32[1,128,128]{2,1,0:T(8,128)S(1)} %get-tuple-element.52), custom_call_target="InvertDiagBlocksLowerTriangular" | custom-call | tf_op jit(solution)/shard_map/jit(cholesky)/cholesky | solution.py:22
  363.9 11.7 %cholesky.544 = f32[128,128]{1,0:T(8,128)S(1)} custom-call(f32[128,128]{1,0:T(8,128)S(1)} %cholesky.606), custom_call_target="Cholesky" | custom-call | tf_op jit(solution)/shard_map/jit(cholesky)/cholesky | solution.py:22
  376.4 9.8 %custom-call.72 = f32[1,128,128]{1,2,0:T(8,128)S(1)} custom-call(f32[1,128,128]{2,1,0:T(8,128)S(1)} %get-tuple-element.50), custom_call_target="InvertDiagBlocksLowerTriangular" | custom-call | tf_op jit(solution)/shard_map/jit(cholesky)/cholesky | solution.py:22
  389.4 11.7 %cholesky.562 = f32[128,128]{1,0:T(8,128)S(1)} custom-call(f32[128,128]{1,0:T(8,128)S(1)} %convolution_subtract_fusion.11), custom_call_target="Cholesky" | custom-call | tf_op jit(solution)/shard_map/jit(cholesky)/cholesky | solution.py:22
  411.5 4.8 select_select_fusion
  416.4 24.1 %while.1 = (s32[]{:T(128)}, f32[1024,1024]{0,1:T(8,128)}, s32[8,2]{0,1:T(2,128)S(1)}, f32[8,128,128]{2,1,0:T(8,128)S(1)}, s32[]{:T(128)}) while((s32[]{:T(128)}, f32[1024,1024]{0,1:T(8,128)}, s32[8,2]{0,1:T(2,128)S(1)}, f32[8,128,128]{2,1,0:T(8,128)S(1)}, s32[]{:T(128)}) %tuple.57), condition=%wide.while_cond, body=%wide.while_body.sunk | while | flops 2 | bytes 393321 | solution.py:36
  440.5 78.8 %custom-call.73 = f32[8,128,128]{1,2,0:T(8,128)S(1)} custom-call(f32[8,128,128]{2,1,0:T(8,128)S(1)} %get-tuple-element.9), custom_call_target="InvertDiagBlocksLowerTriangular" | custom-call | tf_op jit(solution)/shard_map/jit(_solve_triangular)/triangular_solve | solution.py:36
  547.8 5.0 fusion.50
  552.8 5.0 reshape.133
  557.8 141.6 %all-reduce.8.cloned.1.call-done = f32[32,32768]{1,0:T(8,128)} async-done(((f32[32,32768]{1,0:T(8,128)}), f32[32,32768]{1,0:T(8,128)}) %all-reduce.8.cloned.1.call-update) | async-done | bytes 4194320
  712.8 7.5 collective-permute-done.3
  721.9 17.7 %collective-permute-done.4 = bf16[8,32768]{1,0:T(8,128)(2,1)S(1)} collective-permute-done((bf16[8,32768]{1,0:T(8,128)(2,1)S(1)}, bf16[8,32768]{1,0:T(8,128)(2,1)S(1)}, u32[]{:S(2)}, u32[]{:S(2)}) %collective-permute-start.4) | collective-permute-done | bytes 524320 | tf_op jit(solution)/shard_map/ppermute | solution.py:79
  747.9 4.5 copy.51
  752.4 10.2 %fusion.1 = f32[1024,1024]{1,0:T(8,128)} fusion(bf16[1024,1024]{0,1:T(8,128)(2,1)} %collective-permute-done, bf16[1024,1024]{0,1:T(8,128)(2,1)} %copy.51, bf16[1024,1024]{1,0:T(8,128)(2,1)S(1)} %copy-done.3, pred[]{:T(512)S(6)} %eq.22, bf16[1024,1024]{1,0:T(8,128)(2,1)} %copy-done.4), kind=kOutput, calls=%fused_computation.13 | convolution fusion | flops 4300210176 | bytes 12582913 | tf_op jit(solution)/shard_map/dot_general | solution.py:33
  804.7 4.5 fusion.72
  (210 shorter events, 170.6 us)
Async XLA Ops:
  7.2 179.9 %all-reduce.6.cloned.1.call-start = ((), (), s32[]{:S(2)}) async-start(), calls=%async_computation | async-start | bytes 8388608 | tf_op jit(solution)/shard_map/psum | solution.py:50
  14.6 684.9 %all-reduce.8.cloned.1.call-start = ((), (), s32[]{:S(2)}) async-start(), calls=%async_computation.1 | async-start | bytes 8388608
  202.7 1.9 copy-start.2
  252.6 2.0 copy-start
  519.3 23.6 %copy-start.5 = (f32[8,128,128]{1,2,0:T(8,128)}, f32[8,128,128]{1,2,0:T(8,128)S(1)}, u32[]{:S(2)}) copy-start(f32[8,128,128]{1,2,0:T(8,128)S(1)} %custom-call.73) | copy-start | bytes 1572868
  519.3 4.5 copy-start.1
  543.5 9.4 %copy-start.4 = (bf16[1024,1024]{1,0:T(8,128)(2,1)}, bf16[1024,1024]{1,0:T(8,128)(2,1)S(1)}, u32[]{:S(2)}) copy-start(bf16[1024,1024]{1,0:T(8,128)(2,1)S(1)} %fusion.41) | copy-start | bytes 6291460
  543.5 4.4 collective-permute-start
  700.9 5.0 collective-permute-start.1
  706.5 5.0 collective-permute-start.2
  712.0 8.4 %collective-permute-start.3 = (bf16[4,32768]{1,0:T(4,128)(2,1)S(1)}, bf16[4,32768]{1,0:T(4,128)(2,1)S(1)}, u32[]{:S(2)}, u32[]{:S(2)}) collective-permute-start(bf16[4,32768]{1,0:T(4,128)(2,1)S(1)} %maximum_select_fusion.3), channel_id=1, source_target_pairs={{0,4},{1,5},{2,6},{3,7},{4,0},{5,1},{6,2},{7,3},{8,12},{9,13},{10,... | collective-permute-start | bytes 786440 | tf_op jit(solution)/shard_map/ppermute | solution.py:79
  720.8 18.8 %collective-permute-start.4 = (bf16[8,32768]{1,0:T(8,128)(2,1)S(1)}, bf16[8,32768]{1,0:T(8,128)(2,1)S(1)}, u32[]{:S(2)}, u32[]{:S(2)}) collective-permute-start(bf16[8,32768]{1,0:T(8,128)(2,1)S(1)} %maximum_select_fusion.2), channel_id=1, source_target_pairs={{0,8},{1,9},{2,10},{3,11},{4,12},{5,13},{6,14},{7,15},{8,0},{9,1},... | collective-permute-start | bytes 1572872 | tf_op jit(solution)/shard_map/ppermute | solution.py:79
  739.8 2.9 collective-permute-start.5
  747.9 4.5 copy-start.3
  752.3 10.2 %copy-start.6 = (f32[8,128,128]{1,2,0:T(8,128)S(1)}, f32[8,128,128]{1,2,0:T(8,128)}, u32[]{:S(2)}) copy-start(f32[8,128,128]{1,2,0:T(8,128)} %copy-done.5) | copy-start | bytes 1572868
  804.6 10.5 %copy-start.10 = (bf16[128,1024]{0,1:T(8,128)(2,1)S(1)}, bf16[128,1024]{0,1:T(8,128)(2,1)}, u32[]{:S(2)}) copy-start(bf16[128,1024]{0,1:T(8,128)(2,1)} %copy.55) | copy-start | bytes 786436
  804.7 10.6 %copy-start.9 = (bf16[128,1024]{0,1:T(8,128)(2,1)S(1)}, bf16[128,1024]{0,1:T(8,128)(2,1)}, u32[]{:S(2)}) copy-start(bf16[128,1024]{0,1:T(8,128)(2,1)} %copy.56) | copy-start | bytes 786436
  804.7 10.7 %copy-start.8 = (bf16[128,1024]{0,1:T(8,128)(2,1)S(1)}, bf16[128,1024]{0,1:T(8,128)(2,1)}, u32[]{:S(2)}) copy-start(bf16[128,1024]{0,1:T(8,128)(2,1)} %copy.57) | copy-start | bytes 786436
  804.7 10.8 %copy-start.7 = (bf16[128,1024]{0,1:T(8,128)(2,1)S(1)}, bf16[128,1024]{0,1:T(8,128)(2,1)}, u32[]{:S(2)}) copy-start(bf16[128,1024]{0,1:T(8,128)(2,1)} %copy.58) | copy-start | bytes 786436
Sparse Core Ops, SparseCore 0:
  14.7 172.3 all-reduce.5
  558.0 141.4 all-reduce.7
